TPU v7x, 256 devices: a whole 4x4x8 slice. The times are simulated.
256 devices in a mesh: ep: 64 (over z, x, core), rep: 4 (over y).
Axes of the slice: x: 4, y: 4, z: 8, core: 2. Of those that a mesh axis runs over, the one named last changes fastest.
Arguments:
- tokens_one: bfloat16 [2048, 7168], P('ep', 'rep'), may hold values from -6 to 6
- tokens_two: bfloat16 [2048, 7168], P('ep', 'rep'), may hold values from -6 to 6
- routes_one: int32 [2048, 8], P('ep'), may hold values from 0 to 63, all different within a row; in each aligned block of 32 rows (0 to 31, 32 to 63, ...) at most 8 rows name the same one
- routes_two: int32 [2048, 8], P('ep'), may hold values from 0 to 63, all different within a row; in each aligned block of 32 rows (0 to 31, 32 to 63, ...) at most 8 rows name the same one
- gates_one: float32 [2048, 8], P('ep'), may hold values from 0.1 to 0.6
- gates_two: float32 [2048, 8], P('ep'), may hold values from 0.1 to 0.6
- place_before: int32 [64], replicated, may hold values from 0 to 63, each once
- swap_flags: int32 [32], replicated, may hold values 0 or 1
- gate_weight: bfloat16 [64, 7168, 1024], P('ep', 'rep'), may hold values from -0.0625 to 0.0625
- up_weight: bfloat16 [64, 7168, 1024], P('ep', 'rep'), may hold values from -0.0625 to 0.0625
- down_weight: bfloat16 [64, 1024, 7168], P('ep', None, 'rep'), may hold values from -0.1875 to 0.1875
Outputs:
- mixed_one: bfloat16 [2048, 7168], P('ep', 'rep')
- mixed_two: bfloat16 [2048, 7168], P('ep', 'rep')
Inputs may be any that keep to these rules, and one draw needn't show every extreme that they name: `routes_one`: in each aligned block of 32 rows (the rows of one index of ep) no expert is named more than 8 times, and in every draw some expert is named exactly 8 times in some block; a row names 8 different experts. `routes_two`: in each aligned block of 32 rows (the rows of one index of ep) no ep index is named more than 8 times, and in every draw some is named exactly 8 times in some block; a row names 8 different ep indices. `place_before`: each ep index appears once.
All inputs are finite; a program needn't handle non-finite values.
Results may differ from a plain program's by a relative error of at most 0.0058.
Values may be sent and summed in bfloat16 or wider, within the bound.
A program may use at most 128 MiB of HBM per device.

v0:
```python
import jax
import jax.numpy as jnp
from jax import lax
from jax.sharding import PartitionSpec as P


def moe_step(tokens, slots, gates, gate_mat, up_mat, down_mat):
    row_count, width_part = tokens.shape
    top_count = slots.shape[1]
    ep_count = lax.axis_size("ep")
    capacity = min(row_count, 2 * row_count * top_count // ep_count)
    slot_total = ep_count * capacity
    indices = jnp.arange(ep_count, dtype=jnp.int32)
    is_named = slots[:, :, None] == indices
    named_count = jnp.sum(is_named.astype(jnp.int32), axis=1)
    earlier = jnp.cumsum(named_count, axis=0) - named_count
    position = jnp.sum(jnp.where(is_named, earlier[:, None, :], 0), axis=2)
    slot_index = slots * capacity + position
    chosen = jnp.any(slot_index[:, :, None] == jnp.arange(slot_total, dtype=jnp.int32), axis=1)
    outgoing = jnp.dot(chosen.astype(jnp.bfloat16).T, tokens, preferred_element_type=jnp.float32)
    outgoing = outgoing.astype(jnp.bfloat16).reshape(ep_count, capacity, width_part)
    incoming = lax.all_to_all(outgoing, "ep", split_axis=0, concat_axis=0, tiled=True).reshape(
        slot_total, width_part
    )
    gate_part = jnp.dot(incoming, gate_mat, preferred_element_type=jnp.float32)
    up_part = jnp.dot(incoming, up_mat, preferred_element_type=jnp.float32)
    gate_sum, up_sum = lax.psum((gate_part, up_part), "rep")
    hidden = (jax.nn.silu(gate_sum) * up_sum).astype(jnp.bfloat16)
    expert_out = jnp.dot(hidden, down_mat, preferred_element_type=jnp.float32).astype(jnp.bfloat16)
    returned = lax.all_to_all(
        expert_out.reshape(ep_count, capacity, width_part),
        "ep",
        split_axis=0,
        concat_axis=0,
        tiled=True,
    )
    returned = returned.reshape(slot_total, width_part)
    gathered_rows = jnp.take(returned, slot_index.reshape(-1), axis=0).reshape(
        row_count, top_count, width_part
    )
    blended = jnp.sum(gates[:, :, None] * gathered_rows.astype(jnp.float32), axis=1)
    return blended.astype(jnp.bfloat16)


def shards(
    tokens_one,
    tokens_two,
    routes_one,
    routes_two,
    gates_one,
    gates_two,
    place_before,
    swap_flags,
    gate_weight,
    up_weight,
    down_weight,
):
    gate_mat = gate_weight[0]
    up_mat = up_weight[0]
    down_mat = down_weight[0]
    ep_count = lax.axis_size("ep")
    half_count = ep_count // 2
    indices = jnp.arange(ep_count, dtype=jnp.int32)
    slots_one = jnp.sum(jnp.where(routes_one[:, :, None] == indices, place_before, 0), axis=2)
    mixed_one = moe_step(tokens_one, slots_one, gates_one, gate_mat, up_mat, down_mat)
    partner = jnp.where(indices < half_count, indices + half_count, indices - half_count)
    flagged = jnp.concatenate([swap_flags, swap_flags]) == 1
    source_two = jnp.where(flagged, partner, indices)
    slots_two = jnp.sum(jnp.where(routes_two[:, :, None] == indices, source_two, 0), axis=2)
    mixed_two = moe_step(tokens_two, slots_two, gates_two, gate_mat, up_mat, down_mat)
    return (mixed_one, mixed_two)


def solution(mesh):
    return jax.shard_map(
        shards,
        mesh=mesh,
        in_specs=(
            P("ep", "rep"),
            P("ep", "rep"),
            P("ep", None),
            P("ep", None),
            P("ep", None),
            P("ep", None),
            P(),
            P(),
            P("ep", "rep", None),
            P("ep", "rep", None),
            P("ep", None, "rep"),
        ),
        out_specs=(P("ep", "rep"), P("ep", "rep")),
        check_vma=False,
    )
```

profile of v0, /device:TPU:2, one launch (start us, length us, event | category | flops | bytes accessed | tf_op | source)
XLA Modules:
  0.0 422.8 jit_solution(15416319657059354151)
XLA Ops:
  7.2 0.0 copy-start
  7.2 0.8 copy.24
  8.0 0.8 compare_select_fusion.3
  8.8 0.7 select_reduce_fusion.1
  9.5 0.1 convert_reduce_fusion
  9.6 0.1 reduce_window_sum.18
  9.7 0.7 select_reduce_fusion
  10.4 0.2 fusion.35
  10.6 0.0 copy-done
  10.6 1.9 fusion.19
  12.5 0.0 copy-start.2
  12.5 0.0 copy-start.5
  12.5 0.0 copy-start.1
  12.5 12.2 %all-to-all-start.2 = ((bf16[64,8,1792]{2,1,0:T(8,128)(2,1)}), bf16[64,8,1792]{2,1,0:T(8,128)(2,1)S(1)}, u32[]{:S(2)}, u32[]{:S(2)}) async-start(bf16[64,8,1792]{2,1,0:T(8,128)(2,1)} %fusion.19), calls=%async_computation.2 | async-start | bytes 3670016 | tf_op jit(solution)/shard_map/all_to_all | solution.py:22
  24.7 0.0 copy-done.2
  24.7 0.1 copy.22
  24.8 0.0 copy-done.5
  24.8 0.7 select_reduce_fusion.3
  25.5 0.1 convert_reduce_fusion.1
  25.6 0.1 reduce_window_sum.17
  25.7 0.7 select_reduce_fusion.2
  26.4 0.2 fusion.34
  26.6 0.0 copy-done.1
  26.6 1.9 fusion.18
  28.5 41.8 %all-to-all-done.2 = bf16[64,8,1792]{2,1,0:T(8,128)(2,1)S(1)} async-done(((bf16[64,8,1792]{2,1,0:T(8,128)(2,1)}), bf16[64,8,1792]{2,1,0:T(8,128)(2,1)S(1)}, u32[]{:S(2)}, u32[]{:S(2)}) %all-to-all-start.2) | async-done | bytes 1835040 | tf_op jit(solution)/shard_map/all_to_all | solution.py:22
  70.3 5.6 %all-to-all-start = ((bf16[64,8,1792]{2,1,0:T(8,128)(2,1)}), bf16[64,8,1792]{2,1,0:T(8,128)(2,1)}, u32[]{:S(2)}, u32[]{:S(2)}) async-start(bf16[64,8,1792]{2,1,0:T(8,128)(2,1)} %fusion.18), calls=%async_computation | async-start | bytes 3670016 | tf_op jit(solution)/shard_map/all_to_all | solution.py:22
  75.9 0.2 all-reduce.3.cloned.1.call-start
  76.2 0.0 copy-start.6
  76.2 5.6 %fusion.4 = f32[512,1024]{1,0:T(8,128)} fusion(bf16[1,1792,1024]{2,1,0:T(8,128)(2,1)} %param.22, bf16[64,8,1792]{2,1,0:T(8,128)(2,1)S(1)} %all-to-all-done.2), kind=kOutput, calls=%fused_computation.6 | convolution fusion | flops 1879048192 | bytes 7602176 | tf_op jit(solution)/shard_map/dot_general | solution.py:26
  81.8 0.0 copy-done.6
  81.8 3.4 fusion.8
  85.2 36.3 %all-to-all-done = bf16[64,8,1792]{2,1,0:T(8,128)(2,1)} async-done(((bf16[64,8,1792]{2,1,0:T(8,128)(2,1)}), bf16[64,8,1792]{2,1,0:T(8,128)(2,1)}, u32[]{:S(2)}, u32[]{:S(2)}) %all-to-all-start) | async-done | bytes 1835040 | tf_op jit(solution)/shard_map/all_to_all | solution.py:22
  121.5 0.0 copy-start.7
  121.5 6.1 %fusion.10 = f32[512,1024]{1,0:T(8,128)} fusion(bf16[1,1792,1024]{2,1,0:T(8,128)(2,1)} %param.21, bf16[64,8,1792]{2,1,0:T(8,128)(2,1)} %all-to-all-done), kind=kOutput, calls=%fused_computation.12 | convolution fusion | flops 1879048192 | bytes 7602176 | tf_op jit(solution)/shard_map/dot_general | solution.py:25
  127.6 0.0 copy-done.7
  127.6 4.9 %fusion.6 = f32[512,1024]{1,0:T(8,128)} fusion(bf16[1,1792,1024]{2,1,0:T(8,128)(2,1)S(1)} %copy-done.7, bf16[64,8,1792]{2,1,0:T(8,128)(2,1)} %all-to-all-done), kind=kOutput, calls=%fused_computation.8 | convolution fusion | flops 1879048192 | bytes 7602176 | tf_op jit(solution)/shard_map/dot_general | solution.py:26
  132.6 0.0 all-reduce.3.cloned.1.call-update
  132.6 161.9 %all-reduce.3.cloned.1.call-done = (f32[512,1024]{1,0:T(8,128)}, f32[512,1024]{1,0:T(8,128)}, f32[512,1024]{1,0:T(8,128)}, f32[512,1024]{1,0:T(8,128)}) async-done(((f32[512,1024]{1,0:T(8,128)}, f32[512,1024]{1,0:T(8,128)}, f32[512,1024]{1,0:T(8,128)}, f32[512,1024]{1,0:T(8,128)}), (f32[512,1024]{1,0:T(8,128)}, f32[512,1024]{1,0:T(8,128)}, f32[512,1024]{1,0:T(8,128)}, ...) | async-done | bytes 8388624 | tf_op jit(solution)/shard_map/psum | solution.py:27
  294.5 6.9 %fusion.20 = bf16[64,8,1792]{2,1,0:T(8,128)(2,1)} fusion(bf16[1,1024,1792]{2,1,0:T(8,128)(2,1)} %param.23, f32[512,1024]{1,0:T(8,128)} %get-tuple-element.5, f32[512,1024]{1,0:T(8,128)} %get-tuple-element.6), kind=kOutput, calls=%fused_computation.20 | convolution fusion | flops 1883111424 | bytes 9699328 | tf_op jit(solution)/shard_map/dot_general | solution.py:29
  301.4 10.5 %all-to-all-start.3 = ((bf16[64,8,1792]{2,1,0:T(8,128)(2,1)}), bf16[64,8,1792]{2,1,0:T(8,128)(2,1)S(1)}, u32[]{:S(2)}, u32[]{:S(2)}) async-start(bf16[64,8,1792]{2,1,0:T(8,128)(2,1)} %fusion.20), calls=%async_computation.3 | async-start | bytes 3670016 | tf_op jit(solution)/shard_map/all_to_all | solution.py:30
  311.9 6.9 %fusion.23 = bf16[64,8,1792]{2,1,0:T(8,128)(2,1)} fusion(bf16[1,1024,1792]{2,1,0:T(8,128)(2,1)} %param.23, f32[512,1024]{1,0:T(8,128)} %get-tuple-element.3, f32[512,1024]{1,0:T(8,128)} %get-tuple-element.4), kind=kOutput, calls=%fused_computation.21 | convolution fusion | flops 1883111424 | bytes 9699328 | tf_op jit(solution)/shard_map/dot_general | solution.py:29
  318.8 0.0 copy-start.3
  318.8 0.0 copy-start.4
  318.8 38.7 %all-to-all-done.3 = bf16[64,8,1792]{2,1,0:T(8,128)(2,1)S(1)} async-done(((bf16[64,8,1792]{2,1,0:T(8,128)(2,1)}), bf16[64,8,1792]{2,1,0:T(8,128)(2,1)S(1)}, u32[]{:S(2)}, u32[]{:S(2)}) %all-to-all-start.3) | async-done | bytes 1835040 | tf_op jit(solution)/shard_map/all_to_all | solution.py:30
  357.5 5.6 %all-to-all-start.1 = ((bf16[64,8,1792]{2,1,0:T(8,128)(2,1)}), bf16[64,8,1792]{2,1,0:T(8,128)(2,1)}, u32[]{:S(2)}, u32[]{:S(2)}) async-start(bf16[64,8,1792]{2,1,0:T(8,128)(2,1)} %fusion.23), calls=%async_computation.1 | async-start | bytes 3670016 | tf_op jit(solution)/shard_map/all_to_all | solution.py:30
  363.2 0.1 add.53
  363.2 0.1 add.49
  363.3 0.0 copy-done.3
  363.3 0.1 copy.23
  363.4 0.0 copy-done.4
  363.4 0.1 copy.21
  363.6 1.3 gather_fusion.1
  364.9 43.8 %all-to-all-done.1 = bf16[64,8,1792]{2,1,0:T(8,128)(2,1)} async-done(((bf16[64,8,1792]{2,1,0:T(8,128)(2,1)}), bf16[64,8,1792]{2,1,0:T(8,128)(2,1)}, u32[]{:S(2)}, u32[]{:S(2)}) %all-to-all-start.1) | async-done | bytes 1835040 | tf_op jit(solution)/shard_map/all_to_all | solution.py:30
  408.7 3.9 gather_fusion
  412.6 1.7 fusion.26
  414.3 1.7 fusion.27
  (10 shorter events, 0.1 us)
Async XLA Ops:
  7.2 3.4 copy-start
  12.5 12.2 %copy-start.2 = (s32[32,8]{0,1:T(8,128)S(1)}, s32[32,8]{0,1:T(8,128)}, u32[]{:S(2)}) copy-start(s32[32,8]{0,1:T(8,128)} %param.15) | copy-start | bytes 3076
  12.5 12.3 %copy-start.5 = (s32[64]{0:T(128)S(1)}, s32[64]{0:T(128)}, u32[]{:S(2)}) copy-start(s32[64]{0:T(128)} %param.19) | copy-start | bytes 772
  12.5 14.1 %copy-start.1 = (bf16[32,1792]{1,0:T(8,128)(2,1)S(1)}, bf16[32,1792]{1,0:T(8,128)(2,1)}, u32[]{:S(2)}) copy-start(bf16[32,1792]{1,0:T(8,128)(2,1)} %param.13) | copy-start | bytes 344068
  12.5 57.8 %all-to-all-start.2 = ((bf16[64,8,1792]{2,1,0:T(8,128)(2,1)}), bf16[64,8,1792]{2,1,0:T(8,128)(2,1)S(1)}, u32[]{:S(2)}, u32[]{:S(2)}) async-start(bf16[64,8,1792]{2,1,0:T(8,128)(2,1)} %fusion.19), calls=%async_computation.2 | async-start | bytes 3670016 | tf_op jit(solution)/shard_map/all_to_all | solution.py:22
  70.3 51.2 %all-to-all-start = ((bf16[64,8,1792]{2,1,0:T(8,128)(2,1)}), bf16[64,8,1792]{2,1,0:T(8,128)(2,1)}, u32[]{:S(2)}, u32[]{:S(2)}) async-start(bf16[64,8,1792]{2,1,0:T(8,128)(2,1)} %fusion.18), calls=%async_computation | async-start | bytes 3670016 | tf_op jit(solution)/shard_map/all_to_all | solution.py:22
  75.9 218.5 %all-reduce.3.cloned.1.call-start = ((), (), s32[]{:S(2)}) async-start(), calls=%async_computation.4 | async-start | bytes 16777216 | tf_op jit(solution)/shard_map/psum | solution.py:27
  76.2 5.6 %copy-start.6 = (bf16[1,1792,1024]{2,1,0:T(8,128)(2,1)S(1)}, bf16[1,1792,1024]{2,1,0:T(8,128)(2,1)}, u32[]{:S(2)}) copy-start(bf16[1,1792,1024]{2,1,0:T(8,128)(2,1)} %param.21) | copy-start | bytes 11010052
  121.5 6.1 %copy-start.7 = (bf16[1,1792,1024]{2,1,0:T(8,128)(2,1)S(1)}, bf16[1,1792,1024]{2,1,0:T(8,128)(2,1)}, u32[]{:S(2)}) copy-start(bf16[1,1792,1024]{2,1,0:T(8,128)(2,1)} %param.22) | copy-start | bytes 11010052
  301.4 56.2 %all-to-all-start.3 = ((bf16[64,8,1792]{2,1,0:T(8,128)(2,1)}), bf16[64,8,1792]{2,1,0:T(8,128)(2,1)S(1)}, u32[]{:S(2)}, u32[]{:S(2)}) async-start(bf16[64,8,1792]{2,1,0:T(8,128)(2,1)} %fusion.20), calls=%async_computation.3 | async-start | bytes 3670016 | tf_op jit(solution)/shard_map/all_to_all | solution.py:30
  318.8 44.5 %copy-start.3 = (f32[32,8]{0,1:T(8,128)S(1)}, f32[32,8]{0,1:T(8,128)}, u32[]{:S(2)}) copy-start(f32[32,8]{0,1:T(8,128)} %param.18) | copy-start | bytes 3076
  318.8 44.6 %copy-start.4 = (f32[32,8]{0,1:T(8,128)S(1)}, f32[32,8]{0,1:T(8,128)}, u32[]{:S(2)}) copy-start(f32[32,8]{0,1:T(8,128)} %param.17) | copy-start | bytes 3076
  357.5 51.2 %all-to-all-start.1 = ((bf16[64,8,1792]{2,1,0:T(8,128)(2,1)}), bf16[64,8,1792]{2,1,0:T(8,128)(2,1)}, u32[]{:S(2)}, u32[]{:S(2)}) async-start(bf16[64,8,1792]{2,1,0:T(8,128)(2,1)} %fusion.23), calls=%async_computation.1 | async-start | bytes 3670016 | tf_op jit(solution)/shard_map/all_to_all | solution.py:30
Sparse Core Ops, SparseCore 0:
  132.7 161.6 all-reduce.2
where the time goes:
time: 423 us
  waiting for transfers between devices  322 us (76%)
  matrix products  37.8 us (9%)
  starting transfers between devices  34.1 us (8%)
  between operations  14.2 us (3%)
  other arithmetic  7.74 us (2%)
  local copies, waits for them, and re-layouts  6.47 us (2%)
    psum x1, waiting for transfers between devices, moe_step(): gate_sum, up_sum = lax.psum((gate_part, up_part), 'rep')  162 us
    all_to_all x2, waiting for transfers between devices, moe_step(): lax.all_to_all(expert_out.reshape(ep_count, capacity, width_part), 'ep',...  82.5 us
    all_to_all x2, waiting for transfers between devices, moe_step(): lax.all_to_all(outgoing, 'ep', split_axis=0, concat_axis=0, tiled=True)  78.1 us
    all_to_all x2, starting transfers between devices, moe_step(): lax.all_to_all(outgoing, 'ep', split_axis=0, concat_axis=0, tiled=True)  17.7 us
    all_to_all x2, starting transfers between devices, moe_step(): lax.all_to_all(expert_out.reshape(ep_count, capacity, width_part), 'ep',...  16.1 us
    dot_general x2, matrix products, moe_step(): jnp.dot(hidden, down_mat, preferred_element_type=jnp.float32)  13.8 us
    dot_general x2, matrix products, moe_step(): up_part = jnp.dot(incoming, up_mat, preferred_element_type=jnp.float32)  10.5 us
    dot_general x2, matrix products, moe_step(): gate_part = jnp.dot(incoming, gate_mat, preferred_element_type=jnp.float32)  9.57 us
  transfers between devices with their start and end apart: 5, of which 5 were waited for; matrix products, arithmetic and copies ran while one was open for 5% of the time, Pallas kernels for 0%

commit v1 on v0

v1 whole, which is shorter than its diff:
```python
import functools

import jax
import jax.numpy as jnp
from jax import lax
from jax.experimental import pallas as pl
from jax.experimental.pallas import tpu as pltpu
from jax.sharding import PartitionSpec as P

NEAR = 8
MOST = 8
META = 128
HALVES = 2
FAR_ORDER = (0, 1, 7, 2, 6, 3, 5, 4)
ORDER = (
    "S0", "G0", "S1", "S2", "A0", "G1", "D0", "G2", "S3", "A1", "D1",
    "M0", "G3", "A2", "D2", "M1", "F0", "A3", "D3", "M2", "M3", "F1",
)
MESH = pl.DeviceIdType.MESH


def dot(a, b):
    return jnp.dot(a, b, preferred_element_type=jnp.float32)


def dot_nt(a, b):
    return lax.dot_general(a, b, (((1,), (1,)), ((), ())), preferred_element_type=jnp.float32)


def iota(shape, dim):
    return lax.broadcasted_iota(jnp.int32, shape, dim)


def kernel(
    tok_one, tok_two, wg_hbm, wu_hbm, wd_hbm,
    out_one, out_two,
    held, outgo, incoming, part, own, temp, arrived, hidden, expert_out, returned, w_high, w_low, mixed, gathered, kept,
    wg, wu, wd,
    w_sem, a_s, a_r, b_s, b_r, y_s, y_r, h_s, h_r, c_s, c_r, d_s, d_r,
):
    rows, padded = tok_one.shape
    width = padded - META
    fh = wg.shape[1]
    far = held.shape[1] // rows
    reps = arrived.shape[1] + 1
    waves = outgo.shape[0]
    halves = waves // 2
    src_count = far // halves
    n = src_count * rows
    share = src_count * MOST
    total = NEAR * share
    piece = total // reps
    order = FAR_ORDER if far == 8 else tuple(range(far))

    ep = lax.axis_index("ep")
    y = lax.axis_index("rep")
    z = ep // NEAR
    near = lax.rem(ep, NEAR)

    def near_dev(r):
        return (z * NEAR + lax.rem(near + r, NEAR), y)

    def far_dev(r):
        return (lax.rem(z + r + far, far) * NEAR + near, y)

    def rep_dev(r):
        return (ep, lax.rem(y + r, reps))

    def copy(src, dst, send, recv, device):
        return pltpu.make_async_remote_copy(
            src_ref=src, dst_ref=dst, send_sem=send, recv_sem=recv, device_id=device, device_id_type=MESH
        )

    toks = (tok_one, tok_two)
    outs = (out_one, out_two)
    a, b, yy, hh, c, d = {}, {}, {}, {}, {}, {}

    loads = [pltpu.make_async_copy(src, dst, w_sem.at[i]) for i, (src, dst) in enumerate(((wg_hbm, wg), (wu_hbm, wu), (wd_hbm, wd)))]
    for load in loads:
        load.start()

    barrier = pltpu.get_barrier_semaphore()
    partners = [near_dev(r) for r in range(1, NEAR)] + [far_dev(r) for r in range(1, far)] + [rep_dev(r) for r in range(1, reps)]
    for device in partners:
        pl.semaphore_signal(barrier, inc=1, device_id=device, device_id_type=MESH)
    pl.semaphore_wait(barrier, len(partners))

    for step in range(2):
        for k in range(1, far):
            a[step, k] = copy(
                toks[step], held.at[step, pl.ds(k * rows, rows)], a_s.at[step, k - 1], a_r.at[step, k - 1], far_dev(order[k])
            )
            a[step, k].start()
    for step in range(2):
        held[step, 0:rows, :] = toks[step][...]

    def select(w):
        step, half = divmod(w, halves)
        for k in range(half * src_count, (half + 1) * src_count):
            if k:
                a[step, k].wait_recv()
        base = half * n
        meta = held[step, base : base + n, width:padded]
        row_expert = z * NEAR + lax.rem(near + iota((total, META), 0) // share, NEAR)
        pick = jnp.where(iota((total, META), 1) == row_expert, 1.0, 0.0).astype(jnp.bfloat16)
        value = dot_nt(pick, meta)
        same = iota((n, n), 0) // rows == iota((n, n), 1) // rows
        upto = jnp.where(same & (iota((n, n), 0) <= iota((n, n), 1)), 1.0, 0.0).astype(jnp.bfloat16)
        count = dot(jnp.where(value > 0.0, 1.0, 0.0).astype(jnp.bfloat16), upto)
        place = lax.rem(iota((total, n), 0), MOST)
        source = lax.rem(iota((total, n), 0), share) // MOST
        good = (value > 0.0) & (count == (place + 1).astype(jnp.float32)) & (iota((total, n), 1) // rows == source)
        chosen = jnp.where(good, 1.0, 0.0).astype(jnp.bfloat16)
        tile = 256 if width % 256 == 0 else 128

        @pl.loop(0, width // tile)
        def _(j):
            cols = pl.ds(pl.multiple_of(j * tile, tile), tile)
            out = dot(chosen, held[step, base : base + n, cols]).astype(jnp.bfloat16)
            outgo[w, :, cols] = out
            incoming[w, 0:share, cols] = out[0:share]

        for r in range(1, NEAR):
            span = pl.ds(r * share, share)
            b[w, r] = copy(outgo.at[w, span], incoming.at[w, span], b_s.at[w, r - 1], b_r.at[w, r - 1], near_dev(r))
            b[w, r].start()

        col_expert = z * NEAR + lax.rem(near + iota((META, total), 1) // share, NEAR)
        high = jnp.where(iota((META, total), 0) == col_expert, 1.0, 0.0).astype(jnp.bfloat16)
        low = jnp.where(iota((META, total), 0) == col_expert + META // 2, 1.0, 0.0).astype(jnp.bfloat16)
        g_high = dot(meta, high)
        g_low = dot(meta, low)
        below = jnp.where(same & (iota((n, n), 1) <= iota((n, n), 0)), 1.0, 0.0).astype(jnp.bfloat16)
        count = dot(below, jnp.where(g_high > 0.0, 1.0, 0.0).astype(jnp.bfloat16))
        place = lax.rem(iota((n, total), 1), MOST)
        source = lax.rem(iota((n, total), 1), share) // MOST
        good = (g_high > 0.0) & (count == (place + 1).astype(jnp.float32)) & (iota((n, total), 0) // rows == source)
        w_high[w] = jnp.where(good, g_high, 0.0).astype(jnp.bfloat16)
        w_low[w] = jnp.where(good, g_low, 0.0).astype(jnp.bfloat16)

    def gate_up(w):
        if w == 0:
            loads[0].wait()
            loads[1].wait()
        for r in range(1, NEAR):
            b[w, r].wait_recv()
        mine = pl.ds(pl.multiple_of(y * piece, piece), piece)
        tile = 256 if fh % 256 == 0 else 128

        for which, mat in enumerate((wg, wu)):

            @pl.loop(0, fh // tile)
            def _(j, which=which, mat=mat):
                cols = pl.ds(pl.multiple_of(j * tile, tile), tile)
                into = pl.ds(pl.multiple_of(which * fh + j * tile, tile), tile)
                value = dot(incoming[w], mat[:, cols])
                temp[:, 0:tile] = value
                part[w, :, into] = value.astype(jnp.bfloat16)
                own[w, :, into] = temp[mine, 0:tile]

        for r in range(1, reps):
            theirs = pl.ds(pl.multiple_of(lax.rem(y + r, reps) * piece, piece), piece)
            yy[w, r] = copy(part.at[w, theirs], arrived.at[w, r - 1], y_s.at[w, r - 1], y_r.at[w, r - 1], rep_dev(r))
            yy[w, r].start()

    def act(w):
        for r in range(1, reps):
            yy[w, r].wait_recv()
        mine = pl.ds(pl.multiple_of(y * piece, piece), piece)
        tile = 256 if fh % 256 == 0 else 128

        @pl.loop(0, fh // tile)
        def _(j):
            cols = pl.ds(pl.multiple_of(j * tile, tile), tile)
            more = pl.ds(pl.multiple_of(fh + j * tile, tile), tile)
            gate = own[w, :, cols]
            up = own[w, :, more]
            for r in range(reps - 1):
                gate = gate + arrived[w, r, :, cols].astype(jnp.float32)
                up = up + arrived[w, r, :, more].astype(jnp.float32)
            hidden[w, mine, cols] = (gate / (1.0 + jnp.exp(-gate)) * up).astype(jnp.bfloat16)

        for r in range(1, reps):
            hh[w, r] = copy(hidden.at[w, mine], hidden.at[w, mine], h_s.at[w, r - 1], h_r.at[w, r - 1], rep_dev(r))
            hh[w, r].start()

    def down(w):
        if w == 0:
            loads[2].wait()
        for r in range(1, reps):
            hh[w, r].wait_recv()
        tile = 256 if width % 256 == 0 else 128

        @pl.loop(0, width // tile)
        def _(j):
            cols = pl.ds(pl.multiple_of(j * tile, tile), tile)
            out = dot(hidden[w], wd[:, cols]).astype(jnp.bfloat16)
            expert_out[w, :, cols] = out
            returned[w, 0:share, cols] = out[0:share]

        for r in range(1, NEAR):
            span = pl.ds(r * share, share)
            c[w, r] = copy(expert_out.at[w, span], returned.at[w, span], c_s.at[w, r - 1], c_r.at[w, r - 1], near_dev(NEAR - r))
            c[w, r].start()

    def mix(w):
        step, half = divmod(w, halves)
        for r in range(1, NEAR):
            c[w, r].wait_recv()
        tile = 256 if width % 256 == 0 else 128

        @pl.loop(0, width // tile)
        def _(j):
            cols = pl.ds(pl.multiple_of(j * tile, tile), tile)
            value = dot(w_high[w], returned[w, :, cols]) + dot(w_low[w], returned[w, :, cols])
            mixed[w, :, cols] = value.astype(jnp.bfloat16)
            if half == 0:
                kept[step, :, cols] = value[0:rows]

        for k in range(half * src_count, (half + 1) * src_count):
            if k:
                d[step, k] = copy(
                    mixed.at[w, pl.ds((k - half * src_count) * rows, rows)],
                    gathered.at[step, k - 1],
                    d_s.at[step, k - 1],
                    d_r.at[step, k - 1],
                    far_dev(-order[k]),
                )
                d[step, k].start()

    def finish(step):
        for k in range(1, far):
            d[step, k].wait_recv()
        tile = 256 if width % 256 == 0 else 128

        @pl.loop(0, width // tile)
        def _(j):
            cols = pl.ds(pl.multiple_of(j * tile, tile), tile)
            value = kept[step, :, cols]
            for k in range(far - 1):
                value = value + gathered[step, k, :, cols].astype(jnp.float32)
            outs[step][:, cols] = value.astype(jnp.bfloat16)

    stages = {"S": select, "G": gate_up, "A": act, "D": down, "M": mix, "F": finish}
    for name in ORDER:
        stages[name[0]](int(name[1:]))
    for table in (a, b, yy, hh, c, d):
        for item in table.values():
            item.wait_send()


def shards(
    tokens_one,
    tokens_two,
    routes_one,
    routes_two,
    gates_one,
    gates_two,
    place_before,
    swap_flags,
    gate_weight,
    up_weight,
    down_weight,
):
    ep_count = lax.axis_size("ep")
    reps = lax.axis_size("rep")
    half_count = ep_count // 2
    rows, width = tokens_one.shape
    fh = gate_weight.shape[2]
    far = ep_count // NEAR
    indices = jnp.arange(ep_count, dtype=jnp.int32)
    slots_one = jnp.sum(jnp.where(routes_one[:, :, None] == indices, place_before, 0), axis=2)
    partner = jnp.where(indices < half_count, indices + half_count, indices - half_count)
    flagged = jnp.concatenate([swap_flags, swap_flags]) == 1
    source_two = jnp.where(flagged, partner, indices)
    slots_two = jnp.sum(jnp.where(routes_two[:, :, None] == indices, source_two, 0), axis=2)

    def with_meta(tokens, slots, gates):
        lanes = jnp.arange(META, dtype=jnp.int32)
        gate = jnp.sum(jnp.where(slots[:, :, None] == lanes % (META // 2), gates[:, :, None], 0.0), axis=1)
        high = lax.reduce_precision(gate, 8, 7)
        meta = jnp.where(lanes < META // 2, high, gate - high).astype(jnp.bfloat16)
        return jnp.concatenate([tokens, meta], axis=1)

    tok_one = with_meta(tokens_one, slots_one, gates_one)
    tok_two = with_meta(tokens_two, slots_two, gates_two)

    waves = 2 * HALVES
    src_count = far // HALVES
    n = src_count * rows
    total = NEAR * src_count * MOST
    piece = total // reps
    bf16, f32 = jnp.bfloat16, jnp.float32
    dma = pltpu.SemaphoreType.DMA
    vmem = pl.BlockSpec(memory_space=pltpu.VMEM)
    hbm = pl.BlockSpec(memory_space=pl.ANY)
    return pl.pallas_call(
        kernel,
        out_shape=(jax.ShapeDtypeStruct((rows, width), bf16), jax.ShapeDtypeStruct((rows, width), bf16)),
        in_specs=[vmem, vmem, hbm, hbm, hbm],
        out_specs=(vmem, vmem),
        scratch_shapes=[
            pltpu.VMEM((2, far * rows, width + META), bf16),
            pltpu.VMEM((waves, total, width), bf16),
            pltpu.VMEM((waves, total, width), bf16),
            pltpu.VMEM((waves, total, 2 * fh), bf16),
            pltpu.VMEM((waves, piece, 2 * fh), f32),
            pltpu.VMEM((total, 256), f32),
            pltpu.VMEM((waves, reps - 1, piece, 2 * fh), bf16),
            pltpu.VMEM((waves, total, fh), bf16),
            pltpu.VMEM((waves, total, width), bf16),
            pltpu.VMEM((waves, total, width), bf16),
            pltpu.VMEM((waves, n, total), bf16),
            pltpu.VMEM((waves, n, total), bf16),
            pltpu.VMEM((waves, n, width), bf16),
            pltpu.VMEM((2, far - 1, rows, width), bf16),
            pltpu.VMEM((2, rows, width), f32),
            pltpu.VMEM((width, fh), bf16),
            pltpu.VMEM((width, fh), bf16),
            pltpu.VMEM((fh, width), bf16),
            dma((3,)),
            dma((2, far - 1)),
            dma((2, far - 1)),
            dma((waves, NEAR - 1)),
            dma((waves, NEAR - 1)),
            dma((waves, reps - 1)),
            dma((waves, reps - 1)),
            dma((waves, reps - 1)),
            dma((waves, reps - 1)),
            dma((waves, NEAR - 1)),
            dma((waves, NEAR - 1)),
            dma((2, far - 1)),
            dma((2, far - 1)),
        ],
        compiler_params=pltpu.CompilerParams(collective_id=0, has_side_effects=True, vmem_limit_bytes=60 << 20),
    )(tok_one, tok_two, gate_weight[0], up_weight[0], down_weight[0])


def solution(mesh):
    return jax.shard_map(
        shards,
        mesh=mesh,
        in_specs=(
            P("ep", "rep"),
            P("ep", "rep"),
            P("ep", None),
            P("ep", None),
            P("ep", None),
            P("ep", None),
            P(),
            P(),
            P("ep", "rep", None),
            P("ep", "rep", None),
            P("ep", None, "rep"),
        ),
        out_specs=(P("ep", "rep"), P("ep", "rep")),
        check_vma=False,
    )
```

time: 423 us -> 192 us (0.45)
  waiting for transfers between devices: 322 us -> 0 us
  Pallas kernels: 0 us -> 177 us
  matrix products: 37.8 us -> 0 us
  starting transfers between devices: 34.1 us -> 0 us
  between operations: 14.2 us -> 0.66 us
    pallas_call x0 -> x1, Pallas kernels: none -> 177 us  [shards(): pl.pallas_call(kernel, out_shape=(jax.ShapeDtypeStruct((rows, width), bf1...]
    psum x1 -> x0, waiting for transfers between devices: 162 us -> none  [moe_step(): gate_sum, up_sum = lax.psum((gate_part, up_part), 'rep')]
    all_to_all x4 -> x0, waiting for transfers between devices: 161 us -> none  [the longest x2 82.5 us: moe_step(): lax.all_to_all(expert_out.reshape(ep_count, capacity, width_part), 'ep',...]
    dot_general x8 -> x0, matrix products: 37.8 us -> none  [the longest x2 13.8 us: moe_step(): jnp.dot(hidden, down_mat, preferred_element_type=jnp.float32)]
    all_to_all x4 -> x0, starting transfers between devices: 33.9 us -> none  [the longest x2 17.7 us: moe_step(): lax.all_to_all(outgoing, 'ep', split_axis=0, concat_axis=0, tiled=True)]
    reduce_sum x7 -> x1, other arithmetic: 5.63 us -> 0.21 us  [with_meta(): jnp.sum(jnp.where(slots[:, :, None] == lanes % (META // 2), gates[:, :, N...]
    gather x2 -> x0, local copies, waits for them, and re-layouts: 5.23 us -> none  [moe_step(): jnp.take(returned, slot_index.reshape(-1), axis=0)]
    unnamed x20 -> x6, local copies, waits for them, and re-layouts: 1.06 us -> 6.15 us
  transfers between devices with their start and end apart: 5 -> 0, of which waited for: 5 -> 0; matrix products, arithmetic and copies ran while one was open for 5% -> 0% of each run, Pallas kernels for 0% -> 0%
where the time goes in v1:
time: 192 us; the launch traced here: 190 us
  Pallas kernels  177 us (92%)
  local copies, waits for them, and re-layouts  6.15 us (3%)
  other arithmetic  6.02 us (3%)
    pallas_call x1, Pallas kernels, shards(): pl.pallas_call(kernel, out_shape=(jax.ShapeDtypeStruct((rows, width), bf1...  177 us
    unnamed x6, local copies, waits for them, and re-layouts  6.15 us

profile of v1, /device:TPU:2, one launch (start us, length us, event | category | flops | bytes accessed | tf_op | source)
XLA Modules:
  0.0 190.3 jit_solution(10525245471545690920)
XLA Ops:
  0.6 0.8 compare_select_fusion.1
  1.4 0.8 copy.17
  2.2 0.8 copy.19
  3.0 1.9 select_reduce_fusion.1
  4.9 0.8 copy.18
  5.6 0.8 copy.20
  6.4 0.2 select_reduce_fusion
  6.6 1.5 pad_maximum_fusion.1.tok_two
  8.2 1.5 pad_maximum_fusion.tok_one
  9.7 177.5 %shard_map.122 = (bf16[32,1792]{1,0:T(8,128)(2,1)}, bf16[32,1792]{1,0:T(8,128)(2,1)}) custom-call(bf16[32,1920]{1,0:T(8,128)(2,1)} %pad_maximum_fusion.tok_one, bf16[32,1920]{1,0:T(8,128)(2,1)} %pad_maximum_fusion.1.tok_two, bf16[1792,1024]{1,0:T(8,128)(2,1)} %bitcast.3, bf16[1792,1024]{1,0:T(8,128)(2,1)} %bitcast.4, bf16[1024,1792]{1,0:T(8,128)(2,1)} %bitcast.5), custom_call_target="tpu_custom_call" | custom-call | tf_op jit(solution)/shard_map/pallas_call | solution.py:297
  187.2 1.6 copy.23
  188.8 1.6 copy.24
  (3 shorter events, 0.0 us)

commit v2 on v1

v2 whole, which is shorter than its diff:
```python
import functools

import jax
import jax.numpy as jnp
from jax import lax
from jax.experimental import pallas as pl
from jax.experimental.pallas import tpu as pltpu
from jax.sharding import PartitionSpec as P

NEAR = 8
MOST = 8
META = 128
FAR_ORDER = (0, 1, 7, 2, 6, 3, 5, 4)
WAVES = (
    (0, 0, 2), (0, 2, 2), (0, 4, 2), (0, 6, 2),
    (1, 2, 2), (1, 4, 2), (1, 6, 2), (1, 0, 2),
)
ORDER = (
    "H01", "H11", "S1", "S4", "H02", "G1", "H03", "S2", "S7", "H12", "G4", "G2", "S3", "A4",
    "A1", "H13", "S5", "S6", "G3", "G7", "S0", "D1", "D4", "A3", "G6", "A2", "G5", "D3",
    "M1", "M4", "A6", "A7", "D2", "M3", "G0", "M2", "D6", "A5", "D7", "A0", "M6", "D5",
    "D0", "M7", "M5", "M0", "F1", "F0",
)
MESH = pl.DeviceIdType.MESH


def dot(a, b):
    return jnp.dot(a, b, preferred_element_type=jnp.float32)


def dot_nt(a, b):
    return lax.dot_general(a, b, (((1,), (1,)), ((), ())), preferred_element_type=jnp.float32)


def iota(shape, dim):
    return lax.broadcasted_iota(jnp.int32, shape, dim)


def kernel(
    tok_one, tok_two, routes_one, routes_two, gates_one, gates_two, table, wg_hbm, wu_hbm, wd_hbm,
    out_one, out_two,
    held, outgo, incoming, part, own, temp, arrived, hidden, expert_out, returned, w_high, w_low, mixed, gathered, kept,
    wg, wu, wd,
    w_sem, a_s, a_r, b_s, b_r, y_s, y_r, h_s, h_r, c_s, c_r, d_s, d_r,
):
    rows, width = tok_one.shape
    padded = width + META
    fh = wg.shape[1]
    far = len(FAR_ORDER)
    reps = arrived[0].shape[0] + 1
    tile = 256
    slot_of = {r: k for k, r in enumerate(FAR_ORDER)}

    ep = lax.axis_index("ep")
    y = lax.axis_index("rep")
    z = ep // NEAR
    near = lax.rem(ep, NEAR)

    def near_dev(r):
        return (z * NEAR + lax.rem(near + r, NEAR), y)

    def far_dev(r):
        return (lax.rem(z + r + far, far) * NEAR + near, y)

    def rep_dev(r):
        return (ep, lax.rem(y + r, reps))

    def copy(src, dst, send, recv, device):
        return pltpu.make_async_remote_copy(
            src_ref=src, dst_ref=dst, send_sem=send, recv_sem=recv, device_id=device, device_id_type=MESH
        )

    outs = (out_one, out_two)
    a, b, yy, hh, c, d = {}, {}, {}, {}, {}, {}

    first = [
        pltpu.make_async_copy(tok, held.at[step, pl.ds(0, rows), pl.ds(0, width)], w_sem.at[3 + step])
        for step, tok in enumerate((tok_one, tok_two))
    ]
    loads = [
        pltpu.make_async_copy(src, dst, w_sem.at[i])
        for i, (src, dst) in enumerate(((wg_hbm, wg), (wu_hbm, wu), (wd_hbm, wd)))
    ]
    for load in first + loads:
        load.start()

    barrier = pltpu.get_barrier_semaphore()
    partners = [near_dev(r) for r in range(1, NEAR)] + [far_dev(r) for r in range(1, far)]
    partners = partners + [rep_dev(r) for r in range(1, reps)]
    for device in partners:
        pl.semaphore_signal(barrier, inc=1, device_id=device, device_id_type=MESH)

    experts = META // 2
    for step, (routes, gates) in enumerate(((routes_one, gates_one), (routes_two, gates_two))):
        lanes = iota((experts, rows), 0)
        value = jnp.zeros((experts, rows), jnp.float32)
        for k in range(routes.shape[0]):
            value = value + jnp.where(lanes == routes[k : k + 1, :], gates[k : k + 1, :], 0.0)
        high = value.astype(jnp.bfloat16)
        low = (value - high.astype(jnp.float32)).astype(jnp.bfloat16)
        eye = jnp.where(iota((rows, rows), 0) == iota((rows, rows), 1), 1.0, 0.0).astype(jnp.bfloat16)
        high = dot_nt(eye, high).astype(jnp.bfloat16)
        low = dot_nt(eye, low).astype(jnp.bfloat16)
        slot = table[step : step + 1, 0:experts]
        line = iota((META, experts), 0)
        to_high = jnp.where(slot == line, 1.0, 0.0).astype(jnp.bfloat16)
        to_low = jnp.where(slot + experts == line, 1.0, 0.0).astype(jnp.bfloat16)
        meta = dot_nt(high, to_high) + dot_nt(low, to_low)
        held[step, 0:rows, width:padded] = meta.astype(jnp.bfloat16)
    for load in first:
        load.wait()
    pl.semaphore_wait(barrier, len(partners))

    def block(step, r, cut=None):
        at = slot_of[r] * rows
        if cut is None:
            return held.at[step, pl.ds(at, rows)]
        return held.at[step, pl.ds(at + cut * (rows // 2), rows // 2)]

    def hop(step, h):
        cuts = (0, 1) if 2 * h == far else (None, None)
        for way, sign in enumerate((1, -1)):
            src = block(step, (sign * (h - 1)) % far, cuts[way])
            dst = block(step, (sign * h) % far, cuts[way])
            i = 2 * (h - 1) + way
            a[step, h, way] = copy(src, dst, a_s.at[step, i], a_r.at[step, i], far_dev(sign))
            a[step, h, way].start()

    seen = set()

    def landed(step, h):
        if (step, h) not in seen:
            seen.add((step, h))
            for way in range(2):
                a[step, h, way].wait_recv()

    def relay(code):
        step, h = divmod(code, 10)
        landed(step, h)
        hop(step, h + 1)

    def shape_of(w):
        step, base, count = WAVES[w]
        share = count * MOST
        return step, base, count, count * rows, share, NEAR * share, NEAR * share // reps

    def select(w):
        step, base, count, n, share, total, piece = shape_of(w)
        for r in sorted(FAR_ORDER[base : base + count]):
            if r:
                landed(step, min(r, far - r))
        at = base * rows
        meta = held[step, at : at + n, width:padded]
        row_expert = z * NEAR + lax.rem(near + iota((total, META), 0) // share, NEAR)
        pick = jnp.where(iota((total, META), 1) == row_expert, 1.0, 0.0).astype(jnp.bfloat16)
        value = dot_nt(pick, meta)
        same = iota((n, n), 0) // rows == iota((n, n), 1) // rows
        upto = jnp.where(same & (iota((n, n), 0) <= iota((n, n), 1)), 1.0, 0.0).astype(jnp.bfloat16)
        number = dot(jnp.where(value > 0.0, 1.0, 0.0).astype(jnp.bfloat16), upto)
        place = lax.rem(iota((total, n), 0), MOST)
        source = lax.rem(iota((total, n), 0), share) // MOST
        good = (value > 0.0) & (number == (place + 1).astype(jnp.float32)) & (iota((total, n), 1) // rows == source)
        chosen = jnp.where(good, 1.0, 0.0).astype(jnp.bfloat16)

        @pl.loop(0, width // tile)
        def _(j):
            cols = pl.ds(pl.multiple_of(j * tile, tile), tile)
            out = dot(chosen, held[step, at : at + n, cols]).astype(jnp.bfloat16)
            outgo[w][:, cols] = out
            incoming[w][0:share, cols] = out[0:share]

        for r in range(1, NEAR):
            span = pl.ds(r * share, share)
            b[w, r] = copy(outgo[w].at[span], incoming[w].at[span], b_s.at[w, r - 1], b_r.at[w, r - 1], near_dev(r))
            b[w, r].start()

    def weigh(w):
        step, base, count, n, share, total, piece = shape_of(w)
        at = base * rows
        meta = held[step, at : at + n, width:padded]
        same = iota((n, n), 0) // rows == iota((n, n), 1) // rows
        col_expert = z * NEAR + lax.rem(near + iota((META, total), 1) // share, NEAR)
        high = jnp.where(iota((META, total), 0) == col_expert, 1.0, 0.0).astype(jnp.bfloat16)
        low = jnp.where(iota((META, total), 0) == col_expert + META // 2, 1.0, 0.0).astype(jnp.bfloat16)
        g_high = dot(meta, high)
        g_low = dot(meta, low)
        below = jnp.where(same & (iota((n, n), 1) <= iota((n, n), 0)), 1.0, 0.0).astype(jnp.bfloat16)
        number = dot(below, jnp.where(g_high > 0.0, 1.0, 0.0).astype(jnp.bfloat16))
        place = lax.rem(iota((n, total), 1), MOST)
        source = lax.rem(iota((n, total), 1), share) // MOST
        good = (g_high > 0.0) & (number == (place + 1).astype(jnp.float32)) & (iota((n, total), 0) // rows == source)
        w_high[w][...] = jnp.where(good, g_high, 0.0).astype(jnp.bfloat16)
        w_low[w][...] = jnp.where(good, g_low, 0.0).astype(jnp.bfloat16)

    loaded = set()

    def need(i):
        if i not in loaded:
            loads[i].wait()
            loaded.add(i)

    def gate_up(w):
        step, base, count, n, share, total, piece = shape_of(w)
        need(0)
        need(1)
        for r in range(1, NEAR):
            b[w, r].wait_recv()
        mine = pl.ds(pl.multiple_of(y * piece, piece), piece)

        for which, mat in enumerate((wg, wu)):

            @pl.loop(0, fh // tile)
            def _(j, which=which, mat=mat):
                cols = pl.ds(pl.multiple_of(j * tile, tile), tile)
                into = pl.ds(pl.multiple_of(which * fh + j * tile, tile), tile)
                value = dot(incoming[w][...], mat[:, cols])
                temp[0:total, :] = value
                part[w][:, into] = value.astype(jnp.bfloat16)
                own[w][:, into] = temp[mine, :]

        for r in range(1, reps):
            theirs = pl.ds(pl.multiple_of(lax.rem(y + r, reps) * piece, piece), piece)
            yy[w, r] = copy(part[w].at[theirs], arrived[w].at[r - 1], y_s.at[w, r - 1], y_r.at[w, r - 1], rep_dev(r))
            yy[w, r].start()
        weigh(w)

    def act(w):
        step, base, count, n, share, total, piece = shape_of(w)
        for r in range(1, reps):
            yy[w, r].wait_recv()
        mine = pl.ds(pl.multiple_of(y * piece, piece), piece)

        @pl.loop(0, fh // tile)
        def _(j):
            cols = pl.ds(pl.multiple_of(j * tile, tile), tile)
            more = pl.ds(pl.multiple_of(fh + j * tile, tile), tile)
            gate = own[w][:, cols]
            up = own[w][:, more]
            for r in range(reps - 1):
                gate = gate + arrived[w][r, :, cols].astype(jnp.float32)
                up = up + arrived[w][r, :, more].astype(jnp.float32)
            hidden[w][mine, cols] = (gate / (1.0 + jnp.exp(-gate)) * up).astype(jnp.bfloat16)

        for r in range(1, reps):
            hh[w, r] = copy(
                hidden[w].at[mine], hidden[w].at[mine], h_s.at[w, r - 1], h_r.at[w, r - 1], rep_dev(r)
            )
            hh[w, r].start()

    def down(w):
        step, base, count, n, share, total, piece = shape_of(w)
        need(2)
        for r in range(1, reps):
            hh[w, r].wait_recv()

        @pl.loop(0, width // tile)
        def _(j):
            cols = pl.ds(pl.multiple_of(j * tile, tile), tile)
            out = dot(hidden[w][...], wd[:, cols]).astype(jnp.bfloat16)
            expert_out[w][:, cols] = out
            returned[w][0:share, cols] = out[0:share]

        for r in range(1, NEAR):
            span = pl.ds(r * share, share)
            c[w, r] = copy(
                expert_out[w].at[span], returned[w].at[span], c_s.at[w, r - 1], c_r.at[w, r - 1], near_dev(NEAR - r)
            )
            c[w, r].start()

    def mix(w):
        step, base, count, n, share, total, piece = shape_of(w)
        for r in range(1, NEAR):
            c[w, r].wait_recv()

        @pl.loop(0, width // tile)
        def _(j):
            cols = pl.ds(pl.multiple_of(j * tile, tile), tile)
            value = dot(w_high[w][...], returned[w][:, cols]) + dot(w_low[w][...], returned[w][:, cols])
            mixed[w][:, cols] = value.astype(jnp.bfloat16)
            if base == 0:
                kept[step, :, cols] = value[0:rows]

        for k in range(max(base, 1), base + count):
            d[step, k] = copy(
                mixed[w].at[pl.ds((k - base) * rows, rows)],
                gathered.at[step, k - 1],
                d_s.at[step, k - 1],
                d_r.at[step, k - 1],
                far_dev(-FAR_ORDER[k]),
            )
            d[step, k].start()

    def finish(step):
        for k in range(1, far):
            d[step, k].wait_recv()

        @pl.loop(0, width // tile)
        def _(j):
            cols = pl.ds(pl.multiple_of(j * tile, tile), tile)
            value = kept[step, :, cols]
            for k in range(far - 1):
                value = value + gathered[step, k, :, cols].astype(jnp.float32)
            outs[step][:, cols] = value.astype(jnp.bfloat16)

    hop(0, 1)
    hop(1, 1)
    stages = {"H": relay, "S": select, "G": gate_up, "A": act, "D": down, "M": mix, "F": finish}
    for name in ORDER:
        stages[name[0]](int(name[1:]))
    for copies in (a, b, yy, hh, c, d):
        for item in copies.values():
            item.wait_send()


def shards(
    tokens_one,
    tokens_two,
    routes_one,
    routes_two,
    gates_one,
    gates_two,
    place_before,
    swap_flags,
    gate_weight,
    up_weight,
    down_weight,
):
    ep_count = lax.axis_size("ep")
    reps = lax.axis_size("rep")
    half_count = ep_count // 2
    rows, width = tokens_one.shape
    fh = gate_weight.shape[2]
    far = ep_count // NEAR
    indices = jnp.arange(ep_count, dtype=jnp.int32)
    partner = jnp.where(indices < half_count, indices + half_count, indices - half_count)
    flagged = jnp.concatenate([swap_flags, swap_flags]) == 1
    source_two = jnp.where(flagged, partner, indices)
    table = jnp.stack([place_before, source_two])

    sizes = []
    for step, base, count in WAVES:
        total = NEAR * count * MOST
        sizes.append((count * rows, total, total // reps))
    waves = len(WAVES)
    bf16, f32 = jnp.bfloat16, jnp.float32
    dma = pltpu.SemaphoreType.DMA
    vmem = pl.BlockSpec(memory_space=pltpu.VMEM)
    hbm = pl.BlockSpec(memory_space=pl.ANY)
    return pl.pallas_call(
        kernel,
        out_shape=(jax.ShapeDtypeStruct((rows, width), bf16), jax.ShapeDtypeStruct((rows, width), bf16)),
        in_specs=[hbm, hbm, vmem, vmem, vmem, vmem, vmem, hbm, hbm, hbm],
        out_specs=(vmem, vmem),
        scratch_shapes=[
            pltpu.VMEM((2, far * rows, width + META), bf16),
            [pltpu.VMEM((total, width), bf16) for n, total, piece in sizes],
            [pltpu.VMEM((total, width), bf16) for n, total, piece in sizes],
            [pltpu.VMEM((total, 2 * fh), bf16) for n, total, piece in sizes],
            [pltpu.VMEM((piece, 2 * fh), f32) for n, total, piece in sizes],
            pltpu.VMEM((max(total for n, total, piece in sizes), 256), f32),
            [pltpu.VMEM((reps - 1, piece, 2 * fh), bf16) for n, total, piece in sizes],
            [pltpu.VMEM((total, fh), bf16) for n, total, piece in sizes],
            [pltpu.VMEM((total, width), bf16) for n, total, piece in sizes],
            [pltpu.VMEM((total, width), bf16) for n, total, piece in sizes],
            [pltpu.VMEM((n, total), bf16) for n, total, piece in sizes],
            [pltpu.VMEM((n, total), bf16) for n, total, piece in sizes],
            [pltpu.VMEM((n, width), bf16) for n, total, piece in sizes],
            pltpu.VMEM((2, far - 1, rows, width), bf16),
            pltpu.VMEM((2, rows, width), f32),
            pltpu.VMEM((width, fh), bf16),
            pltpu.VMEM((width, fh), bf16),
            pltpu.VMEM((fh, width), bf16),
            dma((5,)),
            dma((2, far)),
            dma((2, far)),
            dma((waves, NEAR - 1)),
            dma((waves, NEAR - 1)),
            dma((waves, reps - 1)),
            dma((waves, reps - 1)),
            dma((waves, reps - 1)),
            dma((waves, reps - 1)),
            dma((waves, NEAR - 1)),
            dma((waves, NEAR - 1)),
            dma((2, far - 1)),
            dma((2, far - 1)),
        ],
        compiler_params=pltpu.CompilerParams(collective_id=0, has_side_effects=True, vmem_limit_bytes=62 << 20),
    )(
        tokens_one, tokens_two, routes_one.T, routes_two.T, gates_one.T, gates_two.T, table,
        gate_weight[0], up_weight[0], down_weight[0],
    )


def solution(mesh):
    return jax.shard_map(
        shards,
        mesh=mesh,
        in_specs=(
            P("ep", "rep"),
            P("ep", "rep"),
            P("ep", None),
            P("ep", None),
            P("ep", None),
            P("ep", None),
            P(),
            P(),
            P("ep", "rep", None),
            P("ep", "rep", None),
            P("ep", None, "rep"),
        ),
        out_specs=(P("ep", "rep"), P("ep", "rep")),
        check_vma=False,
    )
```

time: 192 us -> 133 us (0.69)
  Pallas kernels: 177 us -> 127 us
  other arithmetic: 6.02 us -> 2.03 us
  local copies, waits for them, and re-layouts: 6.15 us -> 3.1 us
    pallas_call x1, Pallas kernels: 177 us -> 127 us  [shards(): pl.pallas_call(kernel, out_shape=(jax.ShapeDtypeStruct((rows, width), bf1...]
    concatenate x2 -> x0, other arithmetic: 3.09 us -> none  [with_meta(): return jnp.concatenate([tokens, meta], axis=1)]
    unnamed x6 -> x2, local copies, waits for them, and re-layouts: 6.15 us -> 3.1 us
    reduce_sum x2 -> x0, other arithmetic: 2.1 us -> none  [the longest x1 1.9 us: shards(): jnp.sum(jnp.where(routes_two[:, :, None] == indices, source_two, 0), axis=2)]
where the time goes in v2:
time: 133 us
  Pallas kernels  127 us (95%)
  local copies, waits for them, and re-layouts  3.1 us (2%)
  other arithmetic  2.03 us (2%)
    pallas_call x1, Pallas kernels, shards(): pl.pallas_call(kernel, out_shape=(jax.ShapeDtypeStruct((rows, width), bf1...  127 us
    unnamed x2, local copies, waits for them, and re-layouts  3.1 us

profile of v2, /device:TPU:2, one launch (start us, length us, event | category | flops | bytes accessed | tf_op | source)
XLA Modules:
  0.0 133.1 jit_solution(11191263853678953546)
XLA Ops:
  0.6 0.8 compare_select_fusion.1
  1.4 1.2 pad_add_fusion.table
  2.7 127.3 %shard_map.122 = (bf16[32,1792]{1,0:T(8,128)(2,1)}, bf16[32,1792]{1,0:T(8,128)(2,1)}) custom-call(bf16[32,1792]{1,0:T(8,128)(2,1)} %tok_one.1, bf16[32,1792]{1,0:T(8,128)(2,1)} %tok_two.1, s32[8,32]{1,0:T(8,128)} %bitcast.12, s32[8,32]{1,0:T(8,128)} %bitcast.13, f32[8,32]{1,0:T(8,128)} %bitcast.14, f32[8,32]{1,0:T(8,128)} %bitcast.15, ...), custom_call_target="tpu_custom_call" | custom-call | tf_op jit(solution)/shard_map/pallas_call | solution.py:349
  130.0 1.6 %copy.15 = bf16[32,1792]{1,0:T(8,128)(2,1)} copy(bf16[32,1792]{1,0:T(8,128)(2,1)} %get-tuple-element.4) | data formatting | bytes 229376
  131.5 1.6 %copy.16 = bf16[32,1792]{1,0:T(8,128)(2,1)} copy(bf16[32,1792]{1,0:T(8,128)(2,1)} %get-tuple-element.5) | data formatting | bytes 229376

commit v3 on v2

--- a/solution.py
+++ b/solution.py
@@ -16,10 +16,11 @@
     (1, 2, 2), (1, 4, 2), (1, 6, 2), (1, 0, 2),
 )
 ORDER = (
-    "H01", "H11", "S1", "S4", "H02", "G1", "H03", "S2", "S7", "H12", "G4", "G2", "S3", "A4",
-    "A1", "H13", "S5", "S6", "G3", "G7", "S0", "D1", "D4", "A3", "G6", "A2", "G5", "D3",
-    "M1", "M4", "A6", "A7", "D2", "M3", "G0", "M2", "D6", "A5", "D7", "A0", "M6", "D5",
-    "D0", "M7", "M5", "M0", "F1", "F0",
+    "H01", "S0", "H02", "S1", "H11", "G0", "S2", "H03", "H12", "G1", "S3", "R0", "S5", "R1",
+    "G2", "S7", "A1", "H13", "A0", "G3", "S4", "R2", "R3", "X0", "X1", "S6", "A2", "A3",
+    "G5", "D1", "X3", "X2", "G7", "G4", "D3", "R5", "G6", "M1", "D2", "A5", "R6", "M3",
+    "R4", "D0", "X5", "A6", "M2", "R7", "D5", "X6", "A4", "X4", "D6", "A7", "M0", "M5",
+    "X7", "D4", "M6", "D7", "M4", "M7", "F0", "F1",
 )
 MESH = pl.DeviceIdType.MESH
 
@@ -37,9 +38,9 @@
 
 
 def kernel(
-    tok_one, tok_two, routes_one, routes_two, gates_one, gates_two, table, wg_hbm, wu_hbm, wd_hbm,
-    out_one, out_two,
-    held, outgo, incoming, part, own, temp, arrived, hidden, expert_out, returned, w_high, w_low, mixed, gathered, kept,
+    tok_one, tok_two, routes_one, routes_two, gates_one, gates_two, place, flags, wg_hbm, wu_hbm, wd_hbm,
+    out,
+    held, outgo, incoming, part, own, next_own, temp, far_part, arrived, hidden, expert_out, returned, w_high, w_low, mixed, gathered, kept,
     wg, wu, wd,
     w_sem, a_s, a_r, b_s, b_r, y_s, y_r, h_s, h_r, c_s, c_r, d_s, d_r,
 ):
@@ -47,8 +48,9 @@
     padded = width + META
     fh = wg.shape[1]
     far = len(FAR_ORDER)
-    reps = arrived[0].shape[0] + 1
-    tile = 256
+    reps = 4
+    tile = fh // 2
+    wide = width // 2
     slot_of = {r: k for k, r in enumerate(FAR_ORDER)}
 
     ep = lax.axis_index("ep")
@@ -70,7 +72,6 @@
             src_ref=src, dst_ref=dst, send_sem=send, recv_sem=recv, device_id=device, device_id_type=MESH
         )
 
-    outs = (out_one, out_two)
     a, b, yy, hh, c, d = {}, {}, {}, {}, {}, {}
 
     first = [
@@ -91,6 +92,13 @@
         pl.semaphore_signal(barrier, inc=1, device_id=device, device_id_type=MESH)
 
     experts = META // 2
+    half = experts // 2
+    lane = iota((1, experts), 1)
+    twice = jnp.where(iota((half, experts), 0) == lax.rem(iota((half, experts), 1), half), 1.0, 0.0)
+    flagged = jnp.broadcast_to(flags[...].astype(jnp.float32), (8, half))
+    flagged = dot(flagged.astype(jnp.bfloat16), twice.astype(jnp.bfloat16))[0:1, :]
+    moved = jnp.where(flagged > 0.5, jnp.where(lane < half, lane + half, lane - half), lane)
+    slots = (place[...], moved)
     for step, (routes, gates) in enumerate(((routes_one, gates_one), (routes_two, gates_two))):
         lanes = iota((experts, rows), 0)
         value = jnp.zeros((experts, rows), jnp.float32)
@@ -101,7 +109,7 @@
         eye = jnp.where(iota((rows, rows), 0) == iota((rows, rows), 1), 1.0, 0.0).astype(jnp.bfloat16)
         high = dot_nt(eye, high).astype(jnp.bfloat16)
         low = dot_nt(eye, low).astype(jnp.bfloat16)
-        slot = table[step : step + 1, 0:experts]
+        slot = slots[step]
         line = iota((META, experts), 0)
         to_high = jnp.where(slot == line, 1.0, 0.0).astype(jnp.bfloat16)
         to_low = jnp.where(slot + experts == line, 1.0, 0.0).astype(jnp.bfloat16)
@@ -162,9 +170,9 @@
         good = (value > 0.0) & (number == (place + 1).astype(jnp.float32)) & (iota((total, n), 1) // rows == source)
         chosen = jnp.where(good, 1.0, 0.0).astype(jnp.bfloat16)
 
-        @pl.loop(0, width // tile)
+        @pl.loop(0, width // wide)
         def _(j):
-            cols = pl.ds(pl.multiple_of(j * tile, tile), tile)
+            cols = pl.ds(pl.multiple_of(j * wide, 128), wide)
             out = dot(chosen, held[step, at : at + n, cols]).astype(jnp.bfloat16)
             outgo[w][:, cols] = out
             incoming[w][0:share, cols] = out[0:share]
@@ -217,17 +225,37 @@
                 temp[0:total, :] = value
                 part[w][:, into] = value.astype(jnp.bfloat16)
                 own[w][:, into] = temp[mine, :]
-
-        for r in range(1, reps):
-            theirs = pl.ds(pl.multiple_of(lax.rem(y + r, reps) * piece, piece), piece)
-            yy[w, r] = copy(part[w].at[theirs], arrived[w].at[r - 1], y_s.at[w, r - 1], y_r.at[w, r - 1], rep_dev(r))
-            yy[w, r].start()
+                next_own[w][:, into] = temp[rows_of(w, (1, reps - 1)[which]), :]
+
+        gates, ups = pl.ds(0, fh), pl.ds(fh, fh)
+        across, after, before = rows_of(w, 2), rows_of(w, 1), rows_of(w, reps - 1)
+        to_rep(w, 0, part[w].at[across, gates], far_part[w].at[0], 1)
+        to_rep(w, 1, part[w].at[across, ups], far_part[w].at[1], reps - 1)
+        to_rep(w, 2, part[w].at[after, ups], arrived[w].at[0, :, ups], 1)
+        to_rep(w, 3, part[w].at[before, gates], arrived[w].at[1, :, gates], reps - 1)
         weigh(w)
 
+    def rows_of(w, r):
+        piece = shape_of(w)[-1]
+        return pl.ds(pl.multiple_of(lax.rem(y + r, reps) * piece, piece), piece)
+
+    def to_rep(w, i, src, dst, r):
+        yy[w, i] = copy(src, dst, y_s.at[w, i], y_r.at[w, i], rep_dev(r))
+        yy[w, i].start()
+
+    def reduce(w):
+        gates, ups = pl.ds(0, fh), pl.ds(fh, fh)
+        for i, (r, cols) in enumerate(((1, gates), (reps - 1, ups))):
+            yy[w, i].wait_recv()
+            line = rows_of(w, r)
+            value = next_own[w][:, cols] + far_part[w][i].astype(jnp.float32)
+            part[w][line, cols] = value.astype(jnp.bfloat16)
+            to_rep(w, 4 + i, part[w].at[line, cols], arrived[w].at[i, :, cols], r)
+
     def act(w):
         step, base, count, n, share, total, piece = shape_of(w)
-        for r in range(1, reps):
-            yy[w, r].wait_recv()
+        for i in range(2, 6):
+            yy[w, i].wait_recv()
         mine = pl.ds(pl.multiple_of(y * piece, piece), piece)
 
         @pl.loop(0, fh // tile)
@@ -236,26 +264,32 @@
             more = pl.ds(pl.multiple_of(fh + j * tile, tile), tile)
             gate = own[w][:, cols]
             up = own[w][:, more]
-            for r in range(reps - 1):
+            for r in range(2):
                 gate = gate + arrived[w][r, :, cols].astype(jnp.float32)
                 up = up + arrived[w][r, :, more].astype(jnp.float32)
             hidden[w][mine, cols] = (gate / (1.0 + jnp.exp(-gate)) * up).astype(jnp.bfloat16)
 
-        for r in range(1, reps):
-            hh[w, r] = copy(
-                hidden[w].at[mine], hidden[w].at[mine], h_s.at[w, r - 1], h_r.at[w, r - 1], rep_dev(r)
-            )
-            hh[w, r].start()
+        share_hidden(w, 0, hidden[w].at[mine], 1)
+        share_hidden(w, 1, hidden[w].at[mine], reps - 1)
+
+    def share_hidden(w, i, ref, r):
+        hh[w, i] = copy(ref, ref, h_s.at[w, i], h_r.at[w, i], rep_dev(r))
+        hh[w, i].start()
+
+    def across(w):
+        for i, r in enumerate((1, reps - 1)):
+            hh[w, i].wait_recv()
+            share_hidden(w, 2 + i, hidden[w].at[rows_of(w, reps - r), pl.ds(i * (fh // 2), fh // 2)], r)
 
     def down(w):
         step, base, count, n, share, total, piece = shape_of(w)
         need(2)
-        for r in range(1, reps):
-            hh[w, r].wait_recv()
-
-        @pl.loop(0, width // tile)
+        for i in range(2, 4):
+            hh[w, i].wait_recv()
+
+        @pl.loop(0, width // wide)
         def _(j):
-            cols = pl.ds(pl.multiple_of(j * tile, tile), tile)
+            cols = pl.ds(pl.multiple_of(j * wide, 128), wide)
             out = dot(hidden[w][...], wd[:, cols]).astype(jnp.bfloat16)
             expert_out[w][:, cols] = out
             returned[w][0:share, cols] = out[0:share]
@@ -272,9 +306,9 @@
         for r in range(1, NEAR):
             c[w, r].wait_recv()
 
-        @pl.loop(0, width // tile)
+        @pl.loop(0, width // wide)
         def _(j):
-            cols = pl.ds(pl.multiple_of(j * tile, tile), tile)
+            cols = pl.ds(pl.multiple_of(j * wide, 128), wide)
             value = dot(w_high[w][...], returned[w][:, cols]) + dot(w_low[w][...], returned[w][:, cols])
             mixed[w][:, cols] = value.astype(jnp.bfloat16)
             if base == 0:
@@ -294,17 +328,17 @@
         for k in range(1, far):
             d[step, k].wait_recv()
 
-        @pl.loop(0, width // tile)
+        @pl.loop(0, width // wide)
         def _(j):
-            cols = pl.ds(pl.multiple_of(j * tile, tile), tile)
+            cols = pl.ds(pl.multiple_of(j * wide, 128), wide)
             value = kept[step, :, cols]
             for k in range(far - 1):
                 value = value + gathered[step, k, :, cols].astype(jnp.float32)
-            outs[step][:, cols] = value.astype(jnp.bfloat16)
+            out[step, :, cols] = value.astype(jnp.bfloat16)
 
     hop(0, 1)
     hop(1, 1)
-    stages = {"H": relay, "S": select, "G": gate_up, "A": act, "D": down, "M": mix, "F": finish}
+    stages = {"H": relay, "S": select, "G": gate_up, "R": reduce, "A": act, "X": across, "D": down, "M": mix, "F": finish}
     for name in ORDER:
         stages[name[0]](int(name[1:]))
     for copies in (a, b, yy, hh, c, d):
@@ -327,16 +361,9 @@
 ):
     ep_count = lax.axis_size("ep")
     reps = lax.axis_size("rep")
-    half_count = ep_count // 2
     rows, width = tokens_one.shape
     fh = gate_weight.shape[2]
     far = ep_count // NEAR
-    indices = jnp.arange(ep_count, dtype=jnp.int32)
-    partner = jnp.where(indices < half_count, indices + half_count, indices - half_count)
-    flagged = jnp.concatenate([swap_flags, swap_flags]) == 1
-    source_two = jnp.where(flagged, partner, indices)
-    table = jnp.stack([place_before, source_two])
-
     sizes = []
     for step, base, count in WAVES:
         total = NEAR * count * MOST
@@ -346,19 +373,21 @@
     dma = pltpu.SemaphoreType.DMA
     vmem = pl.BlockSpec(memory_space=pltpu.VMEM)
     hbm = pl.BlockSpec(memory_space=pl.ANY)
-    return pl.pallas_call(
+    mixed = pl.pallas_call(
         kernel,
-        out_shape=(jax.ShapeDtypeStruct((rows, width), bf16), jax.ShapeDtypeStruct((rows, width), bf16)),
-        in_specs=[hbm, hbm, vmem, vmem, vmem, vmem, vmem, hbm, hbm, hbm],
-        out_specs=(vmem, vmem),
+        out_shape=jax.ShapeDtypeStruct((2, rows, width), bf16),
+        in_specs=[hbm, hbm, vmem, vmem, vmem, vmem, vmem, vmem, hbm, hbm, hbm],
+        out_specs=vmem,
         scratch_shapes=[
             pltpu.VMEM((2, far * rows, width + META), bf16),
             [pltpu.VMEM((total, width), bf16) for n, total, piece in sizes],
             [pltpu.VMEM((total, width), bf16) for n, total, piece in sizes],
             [pltpu.VMEM((total, 2 * fh), bf16) for n, total, piece in sizes],
             [pltpu.VMEM((piece, 2 * fh), f32) for n, total, piece in sizes],
-            pltpu.VMEM((max(total for n, total, piece in sizes), 256), f32),
-            [pltpu.VMEM((reps - 1, piece, 2 * fh), bf16) for n, total, piece in sizes],
+            [pltpu.VMEM((piece, 2 * fh), f32) for n, total, piece in sizes],
+            pltpu.VMEM((max(total for n, total, piece in sizes), fh // 2), f32),
+            [pltpu.VMEM((2, piece, fh), bf16) for n, total, piece in sizes],
+            [pltpu.VMEM((2, piece, 2 * fh), bf16) for n, total, piece in sizes],
             [pltpu.VMEM((total, fh), bf16) for n, total, piece in sizes],
             [pltpu.VMEM((total, width), bf16) for n, total, piece in sizes],
             [pltpu.VMEM((total, width), bf16) for n, total, piece in sizes],
@@ -375,10 +404,10 @@
             dma((2, far)),
             dma((waves, NEAR - 1)),
             dma((waves, NEAR - 1)),
-            dma((waves, reps - 1)),
-            dma((waves, reps - 1)),
-            dma((waves, reps - 1)),
-            dma((waves, reps - 1)),
+            dma((waves, 6)),
+            dma((waves, 6)),
+            dma((waves, 4)),
+            dma((waves, 4)),
             dma((waves, NEAR - 1)),
             dma((waves, NEAR - 1)),
             dma((2, far - 1)),
@@ -386,9 +415,11 @@
         ],
         compiler_params=pltpu.CompilerParams(collective_id=0, has_side_effects=True, vmem_limit_bytes=62 << 20),
     )(
-        tokens_one, tokens_two, routes_one.T, routes_two.T, gates_one.T, gates_two.T, table,
+        tokens_one, tokens_two, routes_one.T, routes_two.T, gates_one.T, gates_two.T,
+        place_before[None, :], swap_flags[None, :],
         gate_weight[0], up_weight[0], down_weight[0],
     )
+    return mixed[0], mixed[1]
 
 
 def solution(mesh):

time: 133 us -> 115 us (0.86); the launches traced: 133 us -> 113 us
  Pallas kernels: 127 us -> 110 us
  other arithmetic: 2.03 us -> 0 us
  local copies, waits for them, and re-layouts: 3.1 us -> 1.65 us
    pallas_call x1, Pallas kernels: 127 us -> 110 us  [shards(): pl.pallas_call(kernel, out_shape=jax.ShapeDtypeStruct((2, rows, width), b...]
    unnamed x2 -> x0, local copies, waits for them, and re-layouts: 3.1 us -> none
    squeeze x0 -> x1, local copies, waits for them, and re-layouts: none -> 1.65 us  [shards(): return (mixed[0], mixed[1])]
where the time goes in v3:
time: 115 us; the launch traced here: 113 us
  Pallas kernels  110 us (96%)
  local copies, waits for them, and re-layouts  1.65 us (1%)
    pallas_call x1, Pallas kernels, shards(): pl.pallas_call(kernel, out_shape=jax.ShapeDtypeStruct((2, rows, width), b...  110 us

profile of v3, /device:TPU:2, one launch (start us, length us, event | category | flops | bytes accessed | tf_op | source)
XLA Modules:
  0.0 112.8 jit_solution(10156564165681440938)
XLA Ops:
  0.6 110.5 %shard_map.122 = bf16[2,32,1792]{2,1,0:T(8,128)(2,1)} custom-call(bf16[32,1792]{1,0:T(8,128)(2,1)} %tok_one.1, bf16[32,1792]{1,0:T(8,128)(2,1)} %tok_two.1, s32[8,32]{1,0:T(8,128)} %bitcast.16, s32[8,32]{1,0:T(8,128)} %bitcast.17, f32[8,32]{1,0:T(8,128)} %bitcast.18, f32[8,32]{1,0:T(8,128)} %bitcast.19, s32[1,64]{1,0:T(1,128)} %bitcast.20, ...), custom_call_target="tpu_custom_call" | custom-call | tf_op jit(solution)/shard_map/pallas_call | solution.py:376
  111.1 1.7 %slice_bitcast_fusion = (bf16[32,1792]{1,0:T(8,128)(2,1)}, bf16[32,1792]{1,0:T(8,128)(2,1)}) fusion(bf16[2,32,1792]{2,1,0:T(8,128)(2,1)} %shard_map.122), kind=kLoop, calls=%fused_computation | loop fusion | bytes 458752 | tf_op jit(solution)/shard_map/squeeze | solution.py:422
